TPU v7x, 32 devices: a whole 2x2x4 slice. The times are simulated.
32 devices in a mesh: groups: 2 (over x), pop: 8 (over z, y), tensor: 2 (over core).
Axes of the slice: x: 2, y: 2, z: 4, core: 2. Of those that a mesh axis runs over, the one named last changes fastest.
Arguments:
- prompts: bfloat16 [48, 8192], P('groups'), parts along dimension 0, may hold values from -6 to 6
- gate_weight: bfloat16 [8192, 14848], P('pop', 'tensor'), may hold values from -0.0625 to 0.0625
- up_weight: bfloat16 [8192, 14848], P('pop', 'tensor'), may hold values from -0.0625 to 0.0625
- down_weight_matrix: bfloat16 [14848, 8192], P('tensor', 'pop'), may hold values from -0.046875 to 0.046875
- gate_in: bfloat16 [16, 8192, 4], P(('groups', 'pop')), parts along dimension 0, may hold values from -6 to 6
- gate_output_factors: bfloat16 [16, 14848, 4], P(('groups', 'pop'), 'tensor'), parts along dimension 0, may hold values from -6 to 6
- up_in: bfloat16 [16, 8192, 4], P(('groups', 'pop')), parts along dimension 0, may hold values from -6 to 6
- up_output_factors: bfloat16 [16, 14848, 4], P(('groups', 'pop'), 'tensor'), parts along dimension 0, may hold values from -6 to 6
- down_input_factors: bfloat16 [16, 14848, 4], P('groups', 'tensor'), parts along dimension 0, may hold values from -6 to 6
- down_out: bfloat16 [16, 8192, 4], P('groups', 'pop'), parts along dimension 0, may hold values from -6 to 6
- label_head: bfloat16 [8192, 128], P('tensor'), may hold values from -0.1875 to 0.1875
- targets: int32 [48], P('groups'), parts along dimension 0, may hold values from 0 to 127
Outputs:
- update: bfloat16 [29696, 8192], P(('groups', 'tensor'), 'pop'), parts along dimension 0
- scores: float32 [16], P(('groups', 'pop')), parts along dimension 0
There are 2 independent parts, one for each index of `groups`. A program takes and returns all parts, laid end to end along the dimension named above; an argument that names none is the same for every part. Nothing has to cross between parts.
All inputs are finite; a program needn't handle non-finite values.
Results may differ from a plain program's by a relative error of at most 0.023.
Values may be sent and summed in bfloat16 or wider, within the bound.
A program may use at most 256 MiB of HBM per device.

v0:
```python
import math
import jax
import jax.numpy as jnp
from jax import lax
from jax.sharding import PartitionSpec as P

noise_scale = 0.2
norm_eps = 1e-06


def scaled_rows(values):
    return values * lax.rsqrt(jnp.mean(values * values, axis=-1, keepdims=True) + norm_eps)


def build_hidden(
    gate_baseline, up_baseline, lowrank_gate, lowrank_up, gate_output_factors, up_output_factors
):
    gate_activation = gate_baseline.astype(jnp.float32)[None] + jnp.einsum(
        "hvw,hpw->hvp", lowrank_gate, gate_output_factors, preferred_element_type=jnp.float32
    )
    upper_bound = up_baseline.astype(jnp.float32)[None] + jnp.einsum(
        "hvw,hpw->hvp", lowrank_up, up_output_factors, preferred_element_type=jnp.float32
    )
    return (jax.nn.silu(gate_activation) * upper_bound).astype(jnp.bfloat16)


def label_terms(logits, targets):
    labels = logits.shape[1]
    picks = targets[:, None] == jnp.arange(labels, dtype=jnp.int32)[None, :]
    picked = jnp.sum(jnp.where(picks, logits, 0.0), axis=1)
    return picked - jnp.log(jnp.sum(jnp.exp(logits), axis=1))


def body(
    prompts,
    gate_weight,
    up_weight,
    down_weight_matrix,
    gate_in,
    gate_output_factors,
    up_in,
    up_output_factors,
    down_input_factors,
    down_out,
    label_head,
    targets,
):
    member = lax.axis_index("pop")
    width = prompts.shape[1]
    in_block = gate_weight.shape[0]
    ffn_half = gate_output_factors.shape[1]
    total_ff = ffn_half * lax.axis_size("tensor")
    members = down_input_factors.shape[0]
    rank = down_input_factors.shape[2]
    prompt_f = prompts.astype(jnp.float32)
    normed = scaled_rows(prompt_f).astype(jnp.bfloat16)
    own_cols = lax.dynamic_slice_in_dim(normed, member * in_block, in_block, 1)
    part_gate = jnp.dot(own_cols, gate_weight, preferred_element_type=jnp.float32)
    part_up = jnp.dot(own_cols, up_weight, preferred_element_type=jnp.float32)
    total_gate, total_up = lax.psum((part_gate, part_up), "pop")
    gate_baseline = total_gate.astype(jnp.bfloat16)
    up_baseline = total_up.astype(jnp.bfloat16)
    in_scale = noise_scale / math.sqrt(width)
    lowrank_gate = (
        in_scale * jnp.einsum("rd,mdk->mrk", normed, gate_in, preferred_element_type=jnp.float32)
    ).astype(jnp.bfloat16)
    lowrank_up = (
        in_scale * jnp.einsum("rd,mdk->mrk", normed, up_in, preferred_element_type=jnp.float32)
    ).astype(jnp.bfloat16)
    down_scale = noise_scale / math.sqrt(total_ff)
    hidden_state = build_hidden(
        gate_baseline, up_baseline, lowrank_gate, lowrank_up, gate_output_factors, up_output_factors
    )
    hidden_portion = lax.all_gather(hidden_state, "pop", axis=0, tiled=True)
    out_piece = down_out.astype(jnp.float32)
    entry_point = jnp.einsum(
        "uaz,zh->uah", hidden_portion, down_weight_matrix, preferred_element_type=jnp.float32
    )
    low_part = down_scale * jnp.einsum(
        "lpq,lqb->lpb", hidden_portion, down_input_factors, preferred_element_type=jnp.float32
    )
    partial_rows = entry_point + jnp.einsum(
        "mrk,mdk->mrd", low_part, out_piece, precision=lax.Precision.HIGHEST
    )
    rows_here = lax.all_to_all(partial_rows, "pop", split_axis=0, concat_axis=2, tiled=True)
    summed = lax.psum(rows_here, "tensor")[0]
    output = prompt_f + summed
    final = scaled_rows(output).astype(jnp.bfloat16)
    half = label_head.shape[0]
    own_half = lax.dynamic_slice_in_dim(final, lax.axis_index("tensor") * half, half, 1)
    logits = lax.psum(jnp.dot(own_half, label_head, preferred_element_type=jnp.float32), "tensor")
    reward = jnp.mean(label_terms(logits, targets))
    rewards = lax.all_gather(reward.reshape(1), "pop", axis=0, tiled=True)
    centre = jnp.mean(rewards)
    spread = jnp.mean((rewards - centre) * (rewards - centre))
    scores = (rewards - centre) * lax.rsqrt(spread + norm_eps)
    weighted = (scores[:, None, None] * down_out.astype(jnp.float32)).astype(jnp.bfloat16)
    update = jnp.einsum(
        "mfk,mdk->fd", down_input_factors, weighted, preferred_element_type=jnp.float32
    ) * (1.0 / math.sqrt(members * rank))
    own_score = lax.dynamic_slice_in_dim(scores, member, 1, 0)
    return (update.astype(jnp.bfloat16), own_score)


def solution(mesh):
    placed = (
        P("groups", None),
        P("pop", "tensor"),
        P("pop", "tensor"),
        P("tensor", "pop"),
        P(("groups", "pop"), None, None),
        P(("groups", "pop"), "tensor", None),
        P(("groups", "pop"), None, None),
        P(("groups", "pop"), "tensor", None),
        P("groups", "tensor", None),
        P("groups", "pop", None),
        P("tensor", None),
        P("groups"),
    )
    return jax.shard_map(
        body,
        mesh=mesh,
        in_specs=placed,
        out_specs=(P(("groups", "tensor"), "pop"), P(("groups", "pop"))),
        check_vma=False,
    )
```

profile of v0, /device:TPU:0, one launch (start us, length us, event | category | flops | bytes accessed | tf_op | source)
XLA Modules:
  0.0 282.1 jit_solution(8416717195286552256)
XLA Ops:
  7.2 1.3 fusion.8
  8.5 1.1 fusion.9
  9.7 7.6 %fusion.21 = f32[24,7424]{1,0:T(8,128)S(1)} fusion(bf16[1024,7424]{1,0:T(8,128)(2,1)} %param.14, bf16[24,8192]{1,0:T(8,128)(2,1)S(1)} %fusion.9, s32[]{:T(128)S(6)} %select_n.13), kind=kOutput, calls=%fused_computation.31 | convolution fusion | flops 364904448 | bytes 15966212 | tf_op jit(solution)/shard_map/dot_general | solution.py:59
  17.2 2.1 copy-done.2
  19.3 2.1 fusion.23
  21.4 80.8 %all-reduce.6 = (bf16[24,7424]{1,0:T(8,128)(2,1)S(1)}, bf16[24,7424]{1,0:T(8,128)(2,1)}) all-reduce(f32[24,7424]{1,0:T(8,128)S(1)} %fusion.23, f32[24,7424]{1,0:T(8,128)S(1)} %fusion.21), channel_id=1, replica_groups=mesh['groups'=2,'pop'=8,'tensor'=2] {'pop'}, use_global_device_ids=true, to_apply=%region_1.0 | all-reduce | flops 356352 | bytes 2138112 | tf_op jit(solution)/shard_map/psum | solution.py:60
  102.2 0.7 convolution_add_fusion.1
  102.9 2.4 fusion.5
  105.3 56.4 %all-gather.3.cloned.1.call-done = bf16[192,7424]{1,0:T(8,128)(2,1)} async-done(((bf16[24,7424]{1,0:T(8,128)(2,1)}), bf16[192,7424]{1,0:T(8,128)(2,1)}) %all-gather.3.cloned.1.call-update) | async-done | bytes 2850832 | tf_op jit(solution)/shard_map/all_gather | solution.py:74
  161.8 2.8 convolution_multiply_fusion
  164.6 7.9 %fusion.1 = f32[8,24,1024]{2,1,0:T(8,128)S(1)} fusion(bf16[8,24,7424]{2,1,0:T(8,128)(2,1)} %bitcast.50, bf16[7424,1024]{1,0:T(8,128)(2,1)} %param.15), kind=kOutput, calls=%fused_computation.2 | convolution fusion | flops 2919235584 | bytes 18841600 | tf_op jit(solution)/shard_map/uaz,zh->uah/dot_general | solution.py:76
  173.1 22.9 %all_to_all.18 = f32[8,24,1024]{2,1,0:T(8,128)S(1)} all-to-all(f32[8,24,1024]{2,1,0:T(8,128)S(1)} %convolution_add_fusion.2), channel_id=1, replica_groups=mesh['groups'=2,'pop'=8,'tensor'=2] {'pop'}, dimensions={0} | all-to-all | bytes 1572864 | tf_op jit(solution)/shard_map/all_to_all | solution.py:85
  196.0 0.9 copy.23
  197.0 0.6 dynamic-slice
  197.7 17.0 %all-reduce.5.cloned.1.call-done = f32[24,8192]{1,0:T(8,128)} async-done(((f32[24,8192]{1,0:T(8,128)}), f32[24,8192]{1,0:T(8,128)}) %all-reduce.5.cloned.1.call-update) | async-done | bytes 786448 | tf_op jit(solution)/shard_map/psum | solution.py:86
  214.6 1.4 multiply_reduce_fusion
  216.3 3.4 %psum.31 = f32[24,128]{1,0:T(8,128)S(1)} all-reduce(f32[24,128]{1,0:T(8,128)S(1)} %fusion.11), channel_id=1, replica_groups=mesh['groups'=2,'pop'=8,'tensor'=2] {'tensor'}, use_global_device_ids=true, to_apply=%region_5.6 | all-reduce | flops 3072 | bytes 24576 | tf_op jit(solution)/shard_map/psum | solution.py:91
  219.9 0.6 subtract_reduce_fusion
  221.2 0.7 dynamic-update-slice
  221.9 21.8 %all-reduce = f32[8]{0:T(128)S(1)} all-reduce(f32[8]{0:T(128)S(1)} %dynamic-update-slice), channel_id=1, replica_groups=mesh['groups'=2,'pop'=8,'tensor'=2] {'pop'}, use_global_device_ids=true, to_apply=%add | all-reduce | flops 8 | bytes 64
  243.7 0.6 reduce_sum.68
  245.0 0.6 multiply_reduce_fusion.1
  246.3 8.0 %fusion.3 = bf16[7424,1024]{0,1:T(8,128)(2,1)} fusion(bf16[8,7424,4]{1,2,0:T(4,128)(2,1)S(1)} %copy-done.8, bf16[8,1024,4]{1,2,0:T(4,128)(2,1)S(1)} %copy-done.5, f32[8]{0:T(128)S(1)} %subtract_multiply_fusion), kind=kOutput, calls=%fused_computation.4 | convolution fusion | flops 501841920 | bytes 15745056 | tf_op jit(solution)/shard_map/mfk,mdk->fd/dot_general | solution.py:98
  254.9 20.4 %copy.20 = bf16[7424,1024]{1,0:T(8,128)(2,1)} copy(bf16[7424,1024]{0,1:T(8,128)(2,1)} %fusion.3) | data formatting | bytes 30408704
  (35 shorter events, 1.8 us)
Async XLA Ops:
  7.2 208.8 %copy-start = (bf16[4096,128]{1,0:T(8,128)(2,1)S(1)}, bf16[4096,128]{1,0:T(8,128)(2,1)}, u32[]{:S(2)}) copy-start(bf16[4096,128]{1,0:T(8,128)(2,1)} %param.22) | copy-start | bytes 3145732
  7.2 154.6 %all-gather.3.cloned.1.call-start = ((), (), s32[]{:S(2)}) async-start(), calls=%async_computation.2 | async-start | bytes 3207168 | tf_op jit(solution)/shard_map/all_gather | solution.py:74
  9.6 9.7 %copy-start.2 = (bf16[1024,7424]{1,0:T(8,128)(2,1)S(1)}, bf16[1024,7424]{1,0:T(8,128)(2,1)}, u32[]{:S(2)}) copy-start(bf16[1024,7424]{1,0:T(8,128)(2,1)} %param.13) | copy-start | bytes 45613060
  19.3 82.9 %copy-start.4 = (bf16[1,8192,4]{1,2,0:T(4,128)(2,1)S(1)}, bf16[1,8192,4]{1,2,0:T(4,128)(2,1)}, u32[]{:S(2)}) copy-start(bf16[1,8192,4]{1,2,0:T(4,128)(2,1)} %param.16) | copy-start | bytes 196612
  19.3 82.9 %copy-start.6 = (bf16[1,7424,4]{1,2,0:T(4,128)(2,1)S(1)}, bf16[1,7424,4]{1,2,0:T(4,128)(2,1)}, u32[]{:S(2)}) copy-start(bf16[1,7424,4]{1,2,0:T(4,128)(2,1)} %param.17) | copy-start | bytes 178180
  19.3 83.5 %copy-start.9 = (bf16[1,8192,4]{1,2,0:T(4,128)(2,1)S(1)}, bf16[1,8192,4]{1,2,0:T(4,128)(2,1)}, u32[]{:S(2)}) copy-start(bf16[1,8192,4]{1,2,0:T(4,128)(2,1)} %param.18) | copy-start | bytes 196612
  19.3 83.6 %copy-start.10 = (bf16[1,7424,4]{1,2,0:T(4,128)(2,1)S(1)}, bf16[1,7424,4]{1,2,0:T(4,128)(2,1)}, u32[]{:S(2)}) copy-start(bf16[1,7424,4]{1,2,0:T(4,128)(2,1)} %param.19) | copy-start | bytes 178180
  105.3 109.4 %all-reduce.5.cloned.1.call-start = ((), (), s32[]{:S(2)}) async-start(), calls=%async_computation.1 | async-start | bytes 1572864 | tf_op jit(solution)/shard_map/psum | solution.py:86
  161.8 10.8 %copy-start.5 = (bf16[8,1024,4]{1,2,0:T(4,128)(2,1)S(1)}, bf16[8,1024,4]{1,2,0:T(4,128)(2,1)}, u32[]{:S(2)}) copy-start(bf16[8,1024,4]{1,2,0:T(4,128)(2,1)} %param.21) | copy-start | bytes 196612
  164.6 32.4 %copy-start.11 = (u32[32]{0:T(128)S(1)}, u32[32]{0:T(128)}, u32[]{:S(2)}) copy-start(u32[32]{0:T(128)} %constant.49) | copy-start | bytes 388
  164.6 50.1 %copy-start.3 = (bf16[24,8192]{1,0:T(8,128)(2,1)S(1)}, bf16[24,8192]{1,0:T(8,128)(2,1)}, u32[]{:S(2)}) copy-start(bf16[24,8192]{1,0:T(8,128)(2,1)} %param.12) | copy-start | bytes 1179652
  164.6 55.1 %copy-start.7 = (s32[24]{0:T(128)S(1)}, s32[24]{0:T(128)}, u32[]{:S(2)}) copy-start(s32[24]{0:T(128)} %param.23) | copy-start | bytes 292
  164.6 81.7 %copy-start.8 = (bf16[8,7424,4]{1,2,0:T(4,128)(2,1)S(1)}, bf16[8,7424,4]{1,2,0:T(4,128)(2,1)}, u32[]{:S(2)}) copy-start(bf16[8,7424,4]{1,2,0:T(4,128)(2,1)} %param.20) | copy-start | bytes 1425412
  254.3 21.0 %copy-start.1 = (bf16[4096,128]{1,0:T(8,128)(2,1)S(1)}, bf16[4096,128]{1,0:T(8,128)(2,1)}, u32[]{:S(2)}) copy-start(bf16[4096,128]{1,0:T(8,128)(2,1)} %param.22) | copy-start | bytes 3145732
Sparse Core Ops, SparseCore 0:
  105.4 56.3 all-gather.2
  197.1 17.4 all-reduce.4
where the time goes:
time: 283 us; the launch traced here: 282 us
  blocking collectives  129 us (46%)
  waiting for transfers between devices  73.5 us (26%)
  matrix products  32.3 us (11%)
  local copies, waits for them, and re-layouts  25.4 us (9%)
  between operations  16.2 us (6%)
  other arithmetic  5.78 us (2%)
    psum x1, blocking collectives, body(): total_gate, total_up = lax.psum((part_gate, part_up), 'pop')  80.8 us
    all_gather x1, waiting for transfers between devices, body(): hidden_portion = lax.all_gather(hidden_state, 'pop', axis=0, tiled=True)  56.4 us
    unnamed x29, local copies, waits for them, and re-layouts  24.8 us
    all_to_all x1, blocking collectives, body(): lax.all_to_all(partial_rows, 'pop', split_axis=0, concat_axis=2, tiled=True)  22.9 us
    unnamed x1, blocking collectives  21.8 us
    psum x1, waiting for transfers between devices, body(): summed = lax.psum(rows_here, 'tensor')[0]  17 us
    dot_general x1, matrix products, body(): jnp.einsum('mfk,mdk->fd', down_input_factors, weighted, preferred_element...  7.97 us
    dot_general x1, matrix products, body(): jnp.einsum('uaz,zh->uah', hidden_portion, down_weight_matrix, preferred_e...  7.93 us
  transfers between devices with their start and end apart: 2, of which 2 were waited for; matrix products, arithmetic and copies ran while one was open for 0% of the time, Pallas kernels for 0%

commit v1 on v0

--- a/solution.py
+++ b/solution.py
@@ -71,7 +71,14 @@
     hidden_state = build_hidden(
         gate_baseline, up_baseline, lowrank_gate, lowrank_up, gate_output_factors, up_output_factors
     )
-    hidden_portion = lax.all_gather(hidden_state, "pop", axis=0, tiled=True)
+    ways, here = (lax.axis_size("pop"), lax.axis_index("pop"))
+    hidden_portion, reach = (hidden_state, 1)
+    while reach < ways:
+        theirs = lax.ppermute(hidden_portion, "pop", [(d, d ^ reach) for d in range(ways)])
+        mine_first = jnp.concatenate([hidden_portion, theirs], axis=0)
+        theirs_first = jnp.concatenate([theirs, hidden_portion], axis=0)
+        hidden_portion = jnp.where(here & reach == 0, mine_first, theirs_first)
+        reach = 2 * reach
     out_piece = down_out.astype(jnp.float32)
     entry_point = jnp.einsum(
         "uaz,zh->uah", hidden_portion, down_weight_matrix, preferred_element_type=jnp.float32

time: 283 us -> 299 us (1.057)
  waiting for transfers between devices: 73.5 us -> 88.5 us
  blocking collectives: 129 us -> 125 us
    ppermute x0 -> x3, waiting for transfers between devices: none -> 71 us  [body(): lax.ppermute(hidden_portion, 'pop', [(d, d ^ reach) for d in range(ways)])]
    all_gather x1 -> x0, waiting for transfers between devices: 56.4 us -> none  [body(): hidden_portion = lax.all_gather(hidden_state, 'pop', axis=0, tiled=True)]
    all_to_all x1, blocking collectives: 22.9 us -> 18.6 us  [body(): lax.all_to_all(partial_rows, 'pop', split_axis=0, concat_axis=2, tiled=True)]
    unnamed x29 -> x25, local copies, waits for them, and re-layouts: 24.8 us -> 24.9 us
  transfers between devices with their start and end apart: 2 -> 4, of which waited for: 2 -> 4; matrix products, arithmetic and copies ran while one was open for 0% -> 0% of each run, Pallas kernels for 0% -> 0%
where the time goes in v1:
time: 299 us; the launch traced here: 298 us
  blocking collectives  125 us (42%)
  waiting for transfers between devices  88.5 us (30%)
  matrix products  33.2 us (11%)
  local copies, waits for them, and re-layouts  25.5 us (9%)
  between operations  16.2 us (5%)
  other arithmetic  7.41 us (2%)
    psum x1, blocking collectives, body(): total_gate, total_up = lax.psum((part_gate, part_up), 'pop')  80.9 us
    ppermute x3, waiting for transfers between devices, body(): lax.ppermute(hidden_portion, 'pop', [(d, d ^ reach) for d in range(ways)])  71 us
    unnamed x25, local copies, waits for them, and re-layouts  24.9 us
    unnamed x1, blocking collectives  21.8 us
    all_to_all x1, blocking collectives, body(): lax.all_to_all(partial_rows, 'pop', split_axis=0, concat_axis=2, tiled=True)  18.6 us
    psum x1, waiting for transfers between devices, body(): summed = lax.psum(rows_here, 'tensor')[0]  17.4 us
    dot_general x1, matrix products, body(): jnp.einsum('uaz,zh->uah', hidden_portion, down_weight_matrix, preferred_e...  9.37 us
    dot_general x1, matrix products, body(): jnp.einsum('mfk,mdk->fd', down_input_factors, weighted, preferred_element...  7.96 us
  transfers between devices with their start and end apart: 4, of which 4 were waited for; matrix products, arithmetic and copies ran while one was open for 0% of the time, Pallas kernels for 0%

profile of v1, /device:TPU:0, one launch (start us, length us, event | category | flops | bytes accessed | tf_op | source)
XLA Modules:
  0.0 297.7 jit_solution(7578767713857571869)
XLA Ops:
  7.2 1.3 fusion.12
  8.5 1.1 fusion.13
  9.7 7.6 %fusion.25 = f32[24,7424]{1,0:T(8,128)S(1)} fusion(bf16[1024,7424]{1,0:T(8,128)(2,1)} %param.14, bf16[24,8192]{1,0:T(8,128)(2,1)S(1)} %fusion.13, s32[]{:T(128)S(6)} %select_n.40), kind=kOutput, calls=%fused_computation.35 | convolution fusion | flops 364904448 | bytes 15966212 | tf_op jit(solution)/shard_map/dot_general | solution.py:59
  17.2 2.1 copy-done.2
  19.3 2.1 fusion.27
  21.4 80.9 %all-reduce.6 = (bf16[24,7424]{1,0:T(8,128)(2,1)S(1)}, bf16[24,7424]{1,0:T(8,128)(2,1)}) all-reduce(f32[24,7424]{1,0:T(8,128)S(1)} %fusion.27, f32[24,7424]{1,0:T(8,128)S(1)} %fusion.25), channel_id=1, replica_groups=mesh['groups'=2,'pop'=8,'tensor'=2] {'pop'}, use_global_device_ids=true, to_apply=%region_1.0 | all-reduce | flops 356352 | bytes 2138112 | tf_op jit(solution)/shard_map/psum | solution.py:60
  103.0 1.7 fusion.6
  104.7 1.0 collective-permute-start
  105.7 6.4 %collective-permute-done = bf16[1,24,7424]{2,1,0:T(8,128)(2,1)S(1)} collective-permute-done((bf16[1,24,7424]{2,1,0:T(8,128)(2,1)S(1)}, bf16[1,24,7424]{2,1,0:T(8,128)(2,1)S(1)}, u32[]{:S(2)}, u32[]{:S(2)}) %collective-permute-start) | collective-permute-done | bytes 356384 | tf_op jit(solution)/shard_map/ppermute | solution.py:77
  112.3 16.0 %collective-permute-done.1 = bf16[2,24,7424]{2,1,0:T(8,128)(2,1)} collective-permute-done((bf16[2,24,7424]{2,1,0:T(8,128)(2,1)S(1)}, bf16[2,24,7424]{2,1,0:T(8,128)(2,1)}, u32[]{:S(2)}, u32[]{:S(2)}) %collective-permute-start.1) | collective-permute-done | bytes 712736 | tf_op jit(solution)/shard_map/ppermute | solution.py:77
  128.3 1.5 maximum_select_fusion.1
  129.9 1.1 collective-permute-start.2
  131.0 48.6 %collective-permute-done.2 = bf16[4,24,7424]{2,1,0:T(8,128)(2,1)} collective-permute-done((bf16[4,24,7424]{2,1,0:T(8,128)(2,1)S(1)}, bf16[4,24,7424]{2,1,0:T(8,128)(2,1)}, u32[]{:S(2)}, u32[]{:S(2)}) %collective-permute-start.2) | collective-permute-done | bytes 1425440 | tf_op jit(solution)/shard_map/ppermute | solution.py:77
  179.6 3.0 convolution_multiply_fusion
  183.1 9.4 %fusion.7 = f32[8,24,1024]{2,1,0:T(8,128)S(1)} fusion(f32[8,24,1024]{2,1,0:T(8,128)S(1)} %fusion.38, bf16[7424,1024]{1,0:T(8,128)(2,1)} %param.15, bf16[4,24,7424]{2,1,0:T(8,128)(2,1)} %collective-permute-done.2, bf16[4,24,7424]{2,1,0:T(8,128)(2,1)S(1)} %maximum_select_fusion.1, pred[]{:T(512)S(6)} %eq.25), kind=kOutput, calls=%fused_computation.12 | convolution fusion | flops 2923708416 | bytes 19628032 | tf_op jit(solution)/shard_map/uaz,zh->uah/dot_general | solution.py:83
  192.6 18.6 %all_to_all.18 = f32[8,24,1024]{2,1,0:T(8,128)S(1)} all-to-all(f32[8,24,1024]{2,1,0:T(8,128)S(1)} %fusion.7), channel_id=1, replica_groups=mesh['groups'=2,'pop'=8,'tensor'=2] {'pop'}, dimensions={0} | all-to-all | bytes 1572864 | tf_op jit(solution)/shard_map/all_to_all | solution.py:92
  211.1 0.9 copy.23
  212.7 17.4 %all-reduce.5.cloned.1.call-done = f32[24,8192]{1,0:T(8,128)} async-done(((f32[24,8192]{1,0:T(8,128)}), f32[24,8192]{1,0:T(8,128)}) %all-reduce.5.cloned.1.call-update) | async-done | bytes 786448 | tf_op jit(solution)/shard_map/psum | solution.py:93
  230.2 1.3 multiply_reduce_fusion
  231.9 3.4 %psum.31 = f32[24,128]{1,0:T(8,128)S(1)} all-reduce(f32[24,128]{1,0:T(8,128)S(1)} %fusion.15), channel_id=1, replica_groups=mesh['groups'=2,'pop'=8,'tensor'=2] {'tensor'}, use_global_device_ids=true, to_apply=%region_5.6 | all-reduce | flops 3072 | bytes 24576 | tf_op jit(solution)/shard_map/psum | solution.py:98
  236.7 0.7 dynamic-update-slice
  237.4 21.8 %all-reduce = f32[8]{0:T(128)S(1)} all-reduce(f32[8]{0:T(128)S(1)} %dynamic-update-slice), channel_id=1, replica_groups=mesh['groups'=2,'pop'=8,'tensor'=2] {'pop'}, use_global_device_ids=true, to_apply=%add | all-reduce | flops 8 | bytes 64
  261.8 8.0 %fusion.3 = bf16[7424,1024]{0,1:T(8,128)(2,1)} fusion(bf16[8,7424,4]{1,2,0:T(4,128)(2,1)S(1)} %copy-done.8, bf16[8,1024,4]{1,2,0:T(4,128)(2,1)S(1)} %copy-done.5, f32[8]{0:T(128)S(1)} %subtract_multiply_fusion), kind=kOutput, calls=%fused_computation.4 | convolution fusion | flops 501841920 | bytes 15745056 | tf_op jit(solution)/shard_map/mfk,mdk->fd/dot_general | solution.py:105
  270.4 20.5 %copy.20 = bf16[7424,1024]{1,0:T(8,128)(2,1)} copy(bf16[7424,1024]{0,1:T(8,128)(2,1)} %fusion.3) | data formatting | bytes 30408704
  (36 shorter events, 5.1 us)
Async XLA Ops:
  7.2 224.4 %copy-start = (bf16[4096,128]{1,0:T(8,128)(2,1)S(1)}, bf16[4096,128]{1,0:T(8,128)(2,1)}, u32[]{:S(2)}) copy-start(bf16[4096,128]{1,0:T(8,128)(2,1)} %param.22) | copy-start | bytes 3145732
  7.2 223.0 %all-reduce.5.cloned.1.call-start = ((), (), s32[]{:S(2)}) async-start(), calls=%async_computation.1 | async-start | bytes 1572864 | tf_op jit(solution)/shard_map/psum | solution.py:93
  9.6 9.7 %copy-start.2 = (bf16[1024,7424]{1,0:T(8,128)(2,1)S(1)}, bf16[1024,7424]{1,0:T(8,128)(2,1)}, u32[]{:S(2)}) copy-start(bf16[1024,7424]{1,0:T(8,128)(2,1)} %param.13) | copy-start | bytes 45613060
  19.3 83.0 %copy-start.4 = (bf16[1,8192,4]{1,2,0:T(4,128)(2,1)S(1)}, bf16[1,8192,4]{1,2,0:T(4,128)(2,1)}, u32[]{:S(2)}) copy-start(bf16[1,8192,4]{1,2,0:T(4,128)(2,1)} %param.16) | copy-start | bytes 196612
  19.3 83.0 %copy-start.6 = (bf16[1,7424,4]{1,2,0:T(4,128)(2,1)S(1)}, bf16[1,7424,4]{1,2,0:T(4,128)(2,1)}, u32[]{:S(2)}) copy-start(bf16[1,7424,4]{1,2,0:T(4,128)(2,1)} %param.17) | copy-start | bytes 178180
  104.7 7.4 %collective-permute-start = (bf16[1,24,7424]{2,1,0:T(8,128)(2,1)S(1)}, bf16[1,24,7424]{2,1,0:T(8,128)(2,1)S(1)}, u32[]{:S(2)}, u32[]{:S(2)}) collective-permute-start(bf16[1,24,7424]{2,1,0:T(8,128)(2,1)S(1)} %fusion.6), channel_id=1, source_target_pairs={{0,2},{2,0},{4,6},{6,4},{8,10},{10,8},{12,14},{14,12},{1,3},{3,1},... | collective-permute-start | bytes 1069064 | tf_op jit(solution)/shard_map/ppermute | solution.py:77
  112.3 16.1 %collective-permute-start.1 = (bf16[2,24,7424]{2,1,0:T(8,128)(2,1)S(1)}, bf16[2,24,7424]{2,1,0:T(8,128)(2,1)}, u32[]{:S(2)}, u32[]{:S(2)}) collective-permute-start(bf16[2,24,7424]{2,1,0:T(8,128)(2,1)S(1)} %maximum_select_fusion.2), channel_id=1, source_target_pairs={{0,4},{2,6},{4,0},{6,2},{8,12},{10,14},{12,8},{14,10},{1,5},{3,7},... | collective-permute-start | bytes 2138120 | tf_op jit(solution)/shard_map/ppermute | solution.py:77
  129.9 49.7 %collective-permute-start.2 = (bf16[4,24,7424]{2,1,0:T(8,128)(2,1)S(1)}, bf16[4,24,7424]{2,1,0:T(8,128)(2,1)}, u32[]{:S(2)}, u32[]{:S(2)}) collective-permute-start(bf16[4,24,7424]{2,1,0:T(8,128)(2,1)S(1)} %maximum_select_fusion.1), channel_id=1, source_target_pairs={{0,8},{2,10},{4,12},{6,14},{8,0},{10,2},{12,4},{14,6},{1,9},{3,11}... | collective-permute-start | bytes 4276232 | tf_op jit(solution)/shard_map/ppermute | solution.py:77
  131.0 51.6 %copy-start.5 = (bf16[8,1024,4]{1,2,0:T(4,128)(2,1)S(1)}, bf16[8,1024,4]{1,2,0:T(4,128)(2,1)}, u32[]{:S(2)}) copy-start(bf16[8,1024,4]{1,2,0:T(4,128)(2,1)} %param.21) | copy-start | bytes 196612
  192.5 19.6 %copy-start.9 = (u32[32]{0:T(128)S(1)}, u32[32]{0:T(128)}, u32[]{:S(2)}) copy-start(u32[32]{0:T(128)} %constant.55) | copy-start | bytes 388
  192.5 37.7 %copy-start.3 = (bf16[24,8192]{1,0:T(8,128)(2,1)S(1)}, bf16[24,8192]{1,0:T(8,128)(2,1)}, u32[]{:S(2)}) copy-start(bf16[24,8192]{1,0:T(8,128)(2,1)} %param.12) | copy-start | bytes 1179652
  211.1 24.1 %copy-start.7 = (s32[24]{0:T(128)S(1)}, s32[24]{0:T(128)}, u32[]{:S(2)}) copy-start(s32[24]{0:T(128)} %param.23) | copy-start | bytes 292
  211.1 50.7 %copy-start.8 = (bf16[8,7424,4]{1,2,0:T(4,128)(2,1)S(1)}, bf16[8,7424,4]{1,2,0:T(4,128)(2,1)}, u32[]{:S(2)}) copy-start(bf16[8,7424,4]{1,2,0:T(4,128)(2,1)} %param.20) | copy-start | bytes 1425412
  270.4 20.5 %copy-start.1 = (bf16[4096,128]{1,0:T(8,128)(2,1)S(1)}, bf16[4096,128]{1,0:T(8,128)(2,1)}, u32[]{:S(2)}) copy-start(bf16[4096,128]{1,0:T(8,128)(2,1)} %param.22) | copy-start | bytes 3145732
Sparse Core Ops, SparseCore 0:
  212.2 17.9 all-reduce.4
